TPU v7x, 256 devices: a whole 4x4x8 slice. The times are simulated.
256 devices in a mesh: section: 4 (over z_lo), rep: 8 (over y, core), tp: 8 (over z_hi, x).
Axes of the slice: x: 4, y: 4, z: 8 (z_hi: 2, z_lo: 4; z = z_hi * 4 + z_lo), core: 2. Of those that a mesh axis runs over, the one named last changes fastest.
Arguments:
- acts: bfloat16 [8, 256, 896], P('rep', None, 'tp'), may hold values from -6 to 6
- cotangent: bfloat16 [8, 256, 896], P('rep', None, 'tp'), may hold values from -8.5 to 8.5
- w_gate: bfloat16 [4, 8, 896, 4864], P('section', 'rep', None, 'tp'), may hold values from -3 to 3
- w_up: bfloat16 [4, 8, 896, 4864], P('section', 'rep', None, 'tp'), may hold values from -3 to 3
- w_down: bfloat16 [4, 8, 4864, 896], P('section', 'rep', 'tp'), may hold values from -4.2 to 4.2
- m_gate: bfloat16 [4, 8, 896, 4864], P('section', 'rep', None, 'tp'), may hold values from -0.099609375 to 0.099609375
- m_up: bfloat16 [4, 8, 896, 4864], P('section', 'rep', None, 'tp'), may hold values from -0.099609375 to 0.099609375
- m_down: bfloat16 [4, 8, 4864, 896], P('section', 'rep', 'tp'), may hold values from -0.099609375 to 0.099609375
- v_gate: bfloat16 [4, 8, 896, 4864], P('section', 'rep', None, 'tp'), may hold values from 0.0009994507 to 0.099609375
- v_up: bfloat16 [4, 8, 896, 4864], P('section', 'rep', None, 'tp'), may hold values from 0.0009994507 to 0.099609375
- v_down: bfloat16 [4, 8, 4864, 896], P('section', 'rep', 'tp'), may hold values from 0.0009994507 to 0.099609375
- steps: int32 [4], P('section'), may hold values from 0 to 999
Outputs:
- section_out: bfloat16 [4, 8, 256, 896], P('section', 'rep', None, 'tp')
- section_in_grad: bfloat16 [4, 8, 256, 896], P('section', 'rep', None, 'tp')
- new_gate: bfloat16 [4, 8, 896, 4864], P('section', 'rep', None, 'tp')
- new_up: bfloat16 [4, 8, 896, 4864], P('section', 'rep', None, 'tp')
- new_down: bfloat16 [4, 8, 4864, 896], P('section', 'rep', 'tp')
All inputs are finite; a program needn't handle non-finite values.
Results may differ from a plain program's by a relative error of at most 0.023.
Values may be sent and summed in bfloat16 or wider, within the bound.
A program may use at most 128 MiB of HBM per device.

v0:
```python
import functools
import math
import jax
import jax.numpy as jnp
from jax import lax
from jax.sharding import PartitionSpec as P

D = 896
FF = 4864
TOK = 128
MB = 2
NORM_EPS = 1e-06
ADAM_EPS = 1e-08
LEARN = 0.3
BETA_ONE = 0.9
BETA_TWO = 0.95


def as_sent(array):
    return jax.tree.map(lambda a: a.astype(jnp.bfloat16) if a.dtype == jnp.float32 else a, array)


def from_behind(array, axis, by):
    peers = lax.axis_size(axis)
    return lax.ppermute(array, axis, [(i, (i + by) % peers) for i in range(peers)])


def passed_along(value, axis, steps):
    count = lax.axis_size(axis)
    first, last = (max(0, -steps), min(count, count - steps))
    return lax.ppermute(value, axis, [(source, source + steps) for source in range(first, last)])


def widen(value):
    return lax.all_gather(value, "tp", axis=1, tiled=True)


def norm_parts(x_full):
    xf = x_full.astype(jnp.float32)
    rms = jnp.sqrt(jnp.mean(xf * xf, axis=1, keepdims=True) + NORM_EPS)
    normed = xf / rms
    normed_b = normed.astype(jnp.bfloat16)
    return (xf, rms, normed, normed_b)


def forward_parts(x_full, wg, wu):
    xf, rms, normed, normed_b = norm_parts(x_full)
    gate = jnp.dot(normed_b, wg, preferred_element_type=jnp.float32) * (1.0 / math.sqrt(D))
    upper = jnp.dot(normed_b, wu, preferred_element_type=jnp.float32) * (1.0 / math.sqrt(D))
    return (xf, rms, normed, normed_b, gate, upper)


def adam_step(weight, first, second, grad):
    m_new = BETA_ONE * first.astype(jnp.float32) + (1.0 - BETA_ONE) * grad
    v_new = BETA_TWO * second.astype(jnp.float32) + (1.0 - BETA_TWO) * grad * grad
    return (weight.astype(jnp.float32) - LEARN * m_new / (jnp.sqrt(v_new) + ADAM_EPS)).astype(
        jnp.bfloat16
    )


def partner_mean(stacked, distance):
    other = jax.tree.map(
        lambda part, own: part.astype(own.dtype),
        from_behind(as_sent(stacked), "rep", distance),
        stacked,
    )
    return ((stacked.astype(jnp.float32) + other.astype(jnp.float32)) * 0.5).astype(jnp.bfloat16)


def contract(left, right, left_dim, right_dim):
    return lax.dot_general(
        left, right, (((left_dim,), (right_dim,)), ((), ())), preferred_element_type=jnp.float32
    )


def on_device(
    acts, cotangent, w_gate, w_up, w_down, m_gate, m_up, m_down, v_gate, v_up, v_down, steps
):
    section = lax.axis_index("section")
    sections = lax.axis_size("section")
    part = lax.axis_index("tp")
    local_width = acts.shape[2]
    wg = w_gate[0, 0]
    wu = w_up[0, 0]
    wd = w_down[0, 0]
    local_hidden = wg.shape[1]
    inv_ff = 1.0 / math.sqrt(FF)
    ticks = MB + sections - 1
    inputs = acts[0].reshape(MB, TOK, local_width)
    cots = cotangent[0].reshape(MB, TOK, local_width)
    saved = jnp.zeros((MB, TOK, D), jnp.bfloat16)
    gate_saved = jnp.zeros((MB, TOK, local_hidden), jnp.float32)
    upper_saved = jnp.zeros((MB, TOK, local_hidden), jnp.float32)
    out_buf = jnp.zeros((MB, TOK, local_width), jnp.bfloat16)
    incoming = jnp.zeros((TOK, local_width), jnp.bfloat16)
    for tick in range(ticks):
        micro = tick - section
        valid = (micro >= 0) & (micro < MB)
        place = jnp.clip(micro, 0, MB - 1)
        first = lax.dynamic_index_in_dim(inputs, place, 0, keepdims=False)
        x_local = jnp.where(section == 0, first, incoming)
        x_full = widen(x_local)
        xf, rms, normed, normed_b, gate, upper = forward_parts(x_full, wg, wu)
        hidden = (jax.nn.silu(gate) * upper).astype(jnp.bfloat16)
        partial_out = jnp.dot(hidden, wd, preferred_element_type=jnp.float32) * inv_ff
        share = lax.psum_scatter(
            partial_out.astype(jnp.bfloat16), "tp", scatter_dimension=1, tiled=True
        ).astype(jnp.float32)
        y_local = (x_local.astype(jnp.float32) + share).astype(jnp.bfloat16)
        if tick < ticks - 1:
            incoming = passed_along(y_local, "section", 1)
        saved = jnp.where(valid, lax.dynamic_update_index_in_dim(saved, x_full, place, 0), saved)
        gate_saved = jnp.where(
            valid, lax.dynamic_update_index_in_dim(gate_saved, gate, place, 0), gate_saved
        )
        upper_saved = jnp.where(
            valid, lax.dynamic_update_index_in_dim(upper_saved, upper, place, 0), upper_saved
        )
        out_buf = jnp.where(
            valid, lax.dynamic_update_index_in_dim(out_buf, y_local, place, 0), out_buf
        )
    acc_gate = jnp.zeros(wg.shape, jnp.float32)
    acc_up = jnp.zeros(wu.shape, jnp.float32)
    acc_down = jnp.zeros(wd.shape, jnp.float32)
    grad_buf = jnp.zeros((MB, TOK, local_width), jnp.bfloat16)
    incoming_back = jnp.zeros((TOK, local_width), jnp.bfloat16)
    for tick in range(ticks):
        micro = tick - (sections - 1 - section)
        valid = (micro >= 0) & (micro < MB)
        place = jnp.clip(micro, 0, MB - 1)
        last_cot = lax.dynamic_index_in_dim(cots, place, 0, keepdims=False)
        dy_local = jnp.where(section == sections - 1, last_cot, incoming_back)
        dy_full = widen(dy_local)
        x_full = lax.dynamic_index_in_dim(saved, place, 0, keepdims=False)
        xf, rms, normed, normed_b = norm_parts(x_full)
        gate = lax.dynamic_index_in_dim(gate_saved, place, 0, keepdims=False)
        upper = lax.dynamic_index_in_dim(upper_saved, place, 0, keepdims=False)
        sig = jax.nn.sigmoid(gate)
        active = gate * sig
        hidden = (active * upper).astype(jnp.bfloat16)
        dh = contract(dy_full, wd, 1, 1) * inv_ff
        dgate = (dh * upper * sig * (1.0 + gate * (1.0 - sig))).astype(jnp.bfloat16)
        dup = (dh * active).astype(jnp.bfloat16)
        acc_down = acc_down + jnp.where(valid, contract(hidden, dy_full, 0, 0) * inv_ff, 0.0)
        acc_gate = acc_gate + jnp.where(
            valid, contract(normed_b, dgate, 0, 0) * (1.0 / math.sqrt(D)), 0.0
        )
        acc_up = acc_up + jnp.where(
            valid, contract(normed_b, dup, 0, 0) * (1.0 / math.sqrt(D)), 0.0
        )
        partial_in = (contract(dgate, wg, 1, 1) + contract(dup, wu, 1, 1)) * (1.0 / math.sqrt(D))
        dnorm_local = lax.psum_scatter(
            partial_in.astype(jnp.bfloat16), "tp", scatter_dimension=1, tiled=True
        ).astype(jnp.float32)
        normed_local = lax.dynamic_slice_in_dim(normed, part * local_width, local_width, 1)
        stat = lax.psum(jnp.sum(dnorm_local * normed_local, axis=1), "tp") / D
        dx_local = (
            dy_local.astype(jnp.float32) + (dnorm_local - normed_local * stat[:, None]) / rms
        ).astype(jnp.bfloat16)
        grad_buf = jnp.where(
            valid, lax.dynamic_update_index_in_dim(grad_buf, dx_local, place, 0), grad_buf
        )
        if tick < ticks - 1:
            incoming_back = passed_along(dx_local, "section", -1)
    new_gate_local = adam_step(wg, m_gate[0, 0], v_gate[0, 0], acc_gate)
    new_up_local = adam_step(wu, m_up[0, 0], v_up[0, 0], acc_up)
    new_down_local = adam_step(wd, m_down[0, 0], v_down[0, 0], acc_down)
    flat_size = wg.shape[0] * wg.shape[1]
    stacked = jnp.stack(
        [
            new_gate_local.reshape(flat_size),
            new_up_local.reshape(flat_size),
            new_down_local.reshape(flat_size),
        ]
    )
    levels = lax.axis_size("rep").bit_length() - 1
    branches = [functools.partial(partner_mean, distance=2**level) for level in range(levels)]
    which = steps[0] % levels
    averaged = lax.switch(which, branches, stacked)
    new_gate = averaged[0].reshape(wg.shape)[None, None]
    new_up = averaged[1].reshape(wu.shape)[None, None]
    new_down = averaged[2].reshape(wd.shape)[None, None]
    section_out = out_buf.reshape(1, 1, MB * TOK, local_width)
    section_in_grad = grad_buf.reshape(1, 1, MB * TOK, local_width)
    return (section_out, section_in_grad, new_gate, new_up, new_down)


def solution(mesh):
    return jax.shard_map(
        on_device,
        mesh=mesh,
        in_specs=(
            P("rep", None, "tp"),
            P("rep", None, "tp"),
            P("section", "rep", None, "tp"),
            P("section", "rep", None, "tp"),
            P("section", "rep", "tp", None),
            P("section", "rep", None, "tp"),
            P("section", "rep", None, "tp"),
            P("section", "rep", "tp", None),
            P("section", "rep", None, "tp"),
            P("section", "rep", None, "tp"),
            P("section", "rep", "tp", None),
            P("section"),
        ),
        out_specs=(
            P("section", "rep", None, "tp"),
            P("section", "rep", None, "tp"),
            P("section", "rep", None, "tp"),
            P("section", "rep", None, "tp"),
            P("section", "rep", "tp", None),
        ),
        check_vma=False,
    )
```

profile of v0, /device:TPU:66, one launch (start us, length us, event | category | flops | bytes accessed | tf_op | source)
XLA Modules:
  0.0 1532.5 jit_solution(6093599195167706535)
XLA Ops:
  9.0 44.1 %all-gather = bf16[1,128,896]{1,2,0:T(8,128)(2,1)S(1)} all-gather(bf16[1,128,112]{1,2,0:T(8,128)(2,1)S(1)} %copy_select_fusion.1), channel_id=2, replica_groups=mesh['section'=4,'rep'=8,'tp'=8] {'tp'}, dimensions={2}, use_global_device_ids=true | all-gather | bytes 258048 | tf_op jit(solution)/shard_map/all_gather | solution.py:35
  59.2 76.5 %reduce-scatter.11.cloned.1.call-done = bf16[128,112]{0,1:T(8,128)(2,1)} async-done(((bf16[128,896]{0,1:T(8,128)(2,1)}), bf16[128,112]{0,1:T(8,128)(2,1)}) %reduce-scatter.11.cloned.1.call-update) | async-done | bytes 28688 | tf_op jit(solution)/shard_map/reduce_scatter | solution.py:106
  142.3 40.6 %all_gather.31 = bf16[128,896]{0,1:T(8,128)(2,1)S(1)} all-gather(bf16[128,112]{0,1:T(8,128)(2,1)S(1)} %bitcast_select_fusion.19), channel_id=1, replica_groups=mesh['section'=4,'rep'=8,'tp'=8] {'tp'}, dimensions={1}, use_global_device_ids=true | all-gather | bytes 258048 | tf_op jit(solution)/shard_map/all_gather | solution.py:35
  187.2 76.0 %reduce-scatter.13.cloned.1.call-done = bf16[128,112]{0,1:T(8,128)(2,1)} async-done(((bf16[128,896]{0,1:T(8,128)(2,1)}), bf16[128,112]{0,1:T(8,128)(2,1)}) %reduce-scatter.13.cloned.1.call-update) | async-done | bytes 28688 | tf_op jit(solution)/shard_map/reduce_scatter | solution.py:106
  269.8 40.6 %all_gather.32 = bf16[128,896]{0,1:T(8,128)(2,1)S(1)} all-gather(bf16[128,112]{0,1:T(8,128)(2,1)S(1)} %bitcast_select_fusion.18), channel_id=1, replica_groups=mesh['section'=4,'rep'=8,'tp'=8] {'tp'}, dimensions={1}, use_global_device_ids=true | all-gather | bytes 258048 | tf_op jit(solution)/shard_map/all_gather | solution.py:35
  315.4 75.3 %reduce-scatter.15.cloned.1.call-done = bf16[128,112]{0,1:T(8,128)(2,1)} async-done(((bf16[128,896]{0,1:T(8,128)(2,1)}), bf16[128,112]{0,1:T(8,128)(2,1)}) %reduce-scatter.15.cloned.1.call-update) | async-done | bytes 28688 | tf_op jit(solution)/shard_map/reduce_scatter | solution.py:106
  394.1 43.8 %all-gather.1 = bf16[1,128,896]{1,2,0:T(8,128)(2,1)} all-gather(bf16[1,128,112]{1,2,0:T(8,128)(2,1)} %copy_select_fusion), channel_id=3, replica_groups=mesh['section'=4,'rep'=8,'tp'=8] {'tp'}, dimensions={2}, use_global_device_ids=true | all-gather | bytes 258048 | tf_op jit(solution)/shard_map/all_gather | solution.py:35
  439.4 44.0 %all_gather.33 = bf16[128,896]{0,1:T(8,128)(2,1)S(1)} all-gather(bf16[128,112]{0,1:T(8,128)(2,1)S(1)} %bitcast_select_fusion.17), channel_id=1, replica_groups=mesh['section'=4,'rep'=8,'tp'=8] {'tp'}, dimensions={1}, use_global_device_ids=true | all-gather | bytes 258048 | tf_op jit(solution)/shard_map/all_gather | solution.py:35
  488.8 74.4 %reduce-scatter.17.cloned.1.call-done = bf16[128,112]{0,1:T(8,128)(2,1)} async-done(((bf16[128,896]{0,1:T(8,128)(2,1)}), bf16[128,112]{0,1:T(8,128)(2,1)}) %reduce-scatter.17.cloned.1.call-update) | async-done | bytes 28688 | tf_op jit(solution)/shard_map/reduce_scatter | solution.py:106
  570.6 41.1 %all_gather.34 = bf16[128,896]{0,1:T(8,128)(2,1)S(1)} all-gather(bf16[128,112]{0,1:T(8,128)(2,1)S(1)} %bitcast_select_fusion.16), channel_id=1, replica_groups=mesh['section'=4,'rep'=8,'tp'=8] {'tp'}, dimensions={1}, use_global_device_ids=true | all-gather | bytes 258048 | tf_op jit(solution)/shard_map/all_gather | solution.py:35
  630.5 69.0 %reduce-scatter.21.cloned.1.call-done = bf16[128,112]{0,1:T(8,128)(2,1)} async-done(((bf16[128,896]{0,1:T(8,128)(2,1)}), bf16[128,112]{0,1:T(8,128)(2,1)}) %reduce-scatter.21.cloned.1.call-update) | async-done | bytes 28688 | tf_op jit(solution)/shard_map/reduce_scatter | solution.py:152
  700.4 24.6 %psum.35 = f32[128]{0:T(128)S(1)} all-reduce(f32[128]{0:T(128)S(1)} %fusion.173), channel_id=1, replica_groups=mesh['section'=4,'rep'=8,'tp'=8] {'tp'}, use_global_device_ids=true, to_apply=%region_13.14 | all-reduce | flops 128 | bytes 1024 | tf_op jit(solution)/shard_map/psum | solution.py:156
  729.2 47.1 %reduce-scatter.19.cloned.1.call-done = bf16[128,112]{0,1:T(8,128)(2,1)} async-done(((bf16[128,896]{0,1:T(8,128)(2,1)}), bf16[128,112]{0,1:T(8,128)(2,1)}) %reduce-scatter.19.cloned.1.call-update) | async-done | bytes 28688 | tf_op jit(solution)/shard_map/reduce_scatter | solution.py:106
  779.1 40.6 %all_gather.36 = bf16[128,896]{0,1:T(8,128)(2,1)S(1)} all-gather(bf16[128,112]{0,1:T(8,128)(2,1)S(1)} %bitcast_select_fusion.15), channel_id=1, replica_groups=mesh['section'=4,'rep'=8,'tp'=8] {'tp'}, dimensions={1}, use_global_device_ids=true | all-gather | bytes 258048 | tf_op jit(solution)/shard_map/all_gather | solution.py:35
  829.7 70.5 %reduce-scatter.23.cloned.1.call-done = bf16[128,112]{0,1:T(8,128)(2,1)} async-done(((bf16[128,896]{0,1:T(8,128)(2,1)}), bf16[128,112]{0,1:T(8,128)(2,1)}) %reduce-scatter.23.cloned.1.call-update) | async-done | bytes 28688 | tf_op jit(solution)/shard_map/reduce_scatter | solution.py:152
  933.3 39.7 %all_gather.37 = bf16[128,896]{0,1:T(8,128)(2,1)S(1)} all-gather(bf16[128,112]{0,1:T(8,128)(2,1)S(1)} %bitcast_select_fusion.14), channel_id=1, replica_groups=mesh['section'=4,'rep'=8,'tp'=8] {'tp'}, dimensions={1}, use_global_device_ids=true | all-gather | bytes 258048 | tf_op jit(solution)/shard_map/all_gather | solution.py:35
  982.6 75.5 %reduce-scatter.25.cloned.1.call-done = bf16[128,112]{0,1:T(8,128)(2,1)} async-done(((bf16[128,896]{0,1:T(8,128)(2,1)}), bf16[128,112]{0,1:T(8,128)(2,1)}) %reduce-scatter.25.cloned.1.call-update) | async-done | bytes 28688 | tf_op jit(solution)/shard_map/reduce_scatter | solution.py:152
  1091.2 40.0 %all_gather.38 = bf16[128,896]{0,1:T(8,128)(2,1)S(1)} all-gather(bf16[128,112]{0,1:T(8,128)(2,1)S(1)} %bitcast_select_fusion.13), channel_id=1, replica_groups=mesh['section'=4,'rep'=8,'tp'=8] {'tp'}, dimensions={1}, use_global_device_ids=true | all-gather | bytes 258048 | tf_op jit(solution)/shard_map/all_gather | solution.py:35
  1140.9 75.4 %reduce-scatter.27.cloned.1.call-done = bf16[128,112]{0,1:T(8,128)(2,1)} async-done(((bf16[128,896]{0,1:T(8,128)(2,1)}), bf16[128,112]{0,1:T(8,128)(2,1)}) %reduce-scatter.27.cloned.1.call-update) | async-done | bytes 28688 | tf_op jit(solution)/shard_map/reduce_scatter | solution.py:152
  1248.7 39.9 %all_gather.39 = bf16[128,896]{0,1:T(8,128)(2,1)S(1)} all-gather(bf16[128,112]{0,1:T(8,128)(2,1)S(1)} %bitcast_select_fusion.12), channel_id=1, replica_groups=mesh['section'=4,'rep'=8,'tp'=8] {'tp'}, dimensions={1}, use_global_device_ids=true | all-gather | bytes 258048 | tf_op jit(solution)/shard_map/all_gather | solution.py:35
  1353.2 138.0 %conditional.2 = (bf16[3,544768]{1,0:T(4,128)(2,1)}, bf16[1,544768]{1,0:T(2,128)(2,1)}, bf16[1,544768]{1,0:T(2,128)(2,1)}, bf16[1,544768]{1,0:T(2,128)(2,1)}, bf...) conditional(s32[]{:T(128)} %clamp.3, ...), branch_computations={%region_30.31_spmd, %region_31.32_spmd, %region_32.33_spmd} | conditional | flops 8171520 | bytes 56655996
  1365.0 81.6 %collective-permute-done.2 = bf16[3,544768]{1,0:T(4,128)(2,1)S(1)} collective-permute-done((bf16[3,544768]{1,0:T(4,128)(2,1)S(1)}, bf16[3,544768]{1,0:T(4,128)(2,1)S(1)}, u32[]{:S(2)}, u32[]{:S(2)}) %collective-permute-start.2) | collective-permute-done | bytes 3268640 | tf_op jit(solution)/shard_map/cond/branch_2_fun/ppermute | solution.py:25
  1449.5 32.6 %fusion.237 = (bf16[544768]{0:T(1024)(128)(2,1)S(1)}, bf16[1,544768]{1,0:T(2,128)(2,1)}, bf16[544768]{0:T(1024)(128)(2,1)}, bf16[1,544768]{1,0:T(2,128)(2,1)}, b...) fusion(bf16[3,544768]{1,0:T(4,128)(2,1)S(1)} %add_multiply_fusion.2), kind=kLoop, calls=%fused_computation.386 | loop fusion | bytes 9805824 | tf_op jit(solution)/shard_map/slice | solution.py:182
  1492.3 31.5 %psum.39 = f32[128]{0:T(128)S(1)} all-reduce(f32[128]{0:T(128)S(1)} %fusion.189), channel_id=1, replica_groups=mesh['section'=4,'rep'=8,'tp'=8] {'tp'}, use_global_device_ids=true, to_apply=%region_29.30 | all-reduce | flops 128 | bytes 1024 | tf_op jit(solution)/shard_map/psum | solution.py:156
  (281 shorter events, 290.8 us)
Async XLA Ops:
  7.2 128.5 %reduce-scatter.11.cloned.1.call-start = ((), (), s32[]{:S(2)}) async-start(), calls=%async_computation.10 | async-start | bytes 258048 | tf_op jit(solution)/shard_map/reduce_scatter | solution.py:106
  59.2 124.3 %copy-start.3 = (bf16[1,1,896,608]{2,3,1,0:T(8,128)(2,1)S(1)}, bf16[1,1,896,608]{2,3,1,0:T(8,128)(2,1)}, u32[]{:S(2)}) copy-start(bf16[1,1,896,608]{2,3,1,0:T(8,128)(2,1)} %param.18) | copy-start | bytes 3268612
  59.2 204.0 %reduce-scatter.13.cloned.1.call-start = ((), (), s32[]{:S(2)}) async-start(), calls=%async_computation.11 | async-start | bytes 258048 | tf_op jit(solution)/shard_map/reduce_scatter | solution.py:106
  136.5 5.8 collective-permute-start.3
  187.1 203.6 %reduce-scatter.15.cloned.1.call-start = ((), (), s32[]{:S(2)}) async-start(), calls=%async_computation.12 | async-start | bytes 258048 | tf_op jit(solution)/shard_map/reduce_scatter | solution.py:106
  264.0 5.8 collective-permute-start.4
  314.6 248.6 %reduce-scatter.17.cloned.1.call-start = ((), (), s32[]{:S(2)}) async-start(), calls=%async_computation.13 | async-start | bytes 258048 | tf_op jit(solution)/shard_map/reduce_scatter | solution.py:106
  391.4 47.2 %collective-permute-start.5 = (bf16[128,112]{0,1:T(8,128)(2,1)S(1)}, bf16[128,112]{0,1:T(8,128)(2,1)S(1)}, u32[]{:S(2)}, u32[]{:S(2)}) collective-permute-start(bf16[128,112]{0,1:T(8,128)(2,1)S(1)} %get-tuple-element.80), channel_id=1, source_target_pairs={{0,64},{64,128},{128,192},{1,65},{65,129},{129,193},{2,66},{66,130... | collective-permute-start | bytes 86024 | tf_op jit(solution)/shard_map/ppermute | solution.py:31
  487.6 212.0 %reduce-scatter.21.cloned.1.call-start = ((), (), s32[]{:S(2)}) async-start(), calls=%async_computation.15 | async-start | bytes 258048 | tf_op jit(solution)/shard_map/reduce_scatter | solution.py:152
  564.0 5.8 collective-permute-start.6
  623.3 152.9 %reduce-scatter.19.cloned.1.call-start = ((), (), s32[]{:S(2)}) async-start(), calls=%async_computation.14 | async-start | bytes 258048 | tf_op jit(solution)/shard_map/reduce_scatter | solution.py:106
  629.0 147.2 %copy-start.19 = (bf16[2,128,112]{1,2,0:T(8,128)(2,1)S(1)}, bf16[2,128,112]{1,2,0:T(8,128)(2,1)}, u32[]{:S(2)}) copy-start(bf16[2,128,112]{1,2,0:T(8,128)(2,1)} %copy-done.18) | copy-start | bytes 172036
  629.0 147.2 %copy-start.29 = (bf16[128,112]{0,1:T(8,128)(2,1)S(1)}, bf16[128,112]{0,1:T(8,128)(2,1)}, u32[]{:S(2)}) copy-start(bf16[128,112]{0,1:T(8,128)(2,1)} %copy-done.28) | copy-start | bytes 86020
  629.0 148.7 %copy-start.39 = (bf16[1,128,112]{1,0,2:T(2,128)(2,1)S(1)}, bf16[1,128,112]{1,0,2:T(2,128)(2,1)}, u32[]{:S(2)}) copy-start(bf16[1,128,112]{1,0,2:T(2,128)(2,1)} %get-tuple-element.115) | copy-start | bytes 86020
  629.0 271.1 %reduce-scatter.23.cloned.1.call-start = ((), (), s32[]{:S(2)}) async-start(), calls=%async_computation.16 | async-start | bytes 258048 | tf_op jit(solution)/shard_map/reduce_scatter | solution.py:152
  725.9 51.8 %collective-permute-start.7 = (bf16[128,112]{0,1:T(8,128)(2,1)S(1)}, bf16[128,112]{0,1:T(8,128)(2,1)}, u32[]{:S(2)}, u32[]{:S(2)}) collective-permute-start(bf16[128,112]{0,1:T(8,128)(2,1)S(1)} %get-tuple-element.76), channel_id=1, source_target_pairs={{64,0},{128,64},{192,128},{65,1},{129,65},{193,129},{66,2},{130,66... | collective-permute-start | bytes 86024 | tf_op jit(solution)/shard_map/ppermute | solution.py:31
  824.0 234.1 %reduce-scatter.25.cloned.1.call-start = ((), (), s32[]{:S(2)}) async-start(), calls=%async_computation.17 | async-start | bytes 258048 | tf_op jit(solution)/shard_map/reduce_scatter | solution.py:152
  926.6 6.1 collective-permute-start.8
  977.0 239.3 %reduce-scatter.27.cloned.1.call-start = ((), (), s32[]{:S(2)}) async-start(), calls=%async_computation.18 | async-start | bytes 258048 | tf_op jit(solution)/shard_map/reduce_scatter | solution.py:152
  982.6 108.0 %copy-start.37 = (bf16[1,128,112]{1,0,2:T(2,128)(2,1)S(1)}, bf16[1,128,112]{1,0,2:T(2,128)(2,1)}, u32[]{:S(2)}) copy-start(bf16[1,128,112]{1,0,2:T(2,128)(2,1)} %get-tuple-element.113) | copy-start | bytes 86020
  1084.5 6.0 collective-permute-start.9
  1135.2 356.1 %reduce-scatter.29.cloned.1.call-start = ((), (), s32[]{:S(2)}) async-start(), calls=%async_computation.19 | async-start | bytes 258048 | tf_op jit(solution)/shard_map/reduce_scatter | solution.py:152
  1242.7 6.0 collective-permute-start.10
  1354.3 92.3 %collective-permute-start.2 = (bf16[3,544768]{1,0:T(4,128)(2,1)S(1)}, bf16[3,544768]{1,0:T(4,128)(2,1)S(1)}, u32[]{:S(2)}, u32[]{:S(2)}) collective-permute-start(bf16[3,544768]{1,0:T(4,128)(2,1)S(1)} %param.2), channel_id=1, source_target_pairs={{0,32},{8,40},{16,48},{24,56},{32,0},{40,8},{48,16},{56,24},{1,33}... | collective-permute-start | bytes 9805832 | tf_op jit(solution)/shard_map/cond/branch_2_fun/ppermute | solution.py:25
  (54 other events, 928.4 us)
Sparse Core Ops, SparseCore 0:
  59.3 76.3 reduce-scatter.10
  187.2 75.9 reduce-scatter.12
  314.7 75.9 reduce-scatter.14
  487.7 75.4 reduce-scatter.16
  623.5 76.0 reduce-scatter.20
  703.1 73.1 reduce-scatter.18
  824.1 76.0 reduce-scatter.22
  977.2 80.9 reduce-scatter.24
  1135.3 80.9 reduce-scatter.26
  1292.2 80.7 reduce-scatter.28
where the time goes:
time: 1540 us; the launch traced here: 1530 us
  waiting for transfers between devices  729 us (47%)
  blocking collectives  544 us (35%)
  local copies, waits for them, and re-layouts  88.1 us (6%)
  matrix products  87.2 us (6%)
  starting transfers between devices  34.7 us (2%)
  other arithmetic  32.1 us (2%)
  between operations  16 us (1%)
    all_gather x10, blocking collectives, widen(): return lax.all_gather(value, 'tp', axis=1, tiled=True)  414 us
    reduce_scatter x5, waiting for transfers between devices, on_device(): lax.psum_scatter(partial_out.astype(jnp.bfloat16), 'tp', scatter_dimensio...  349 us
    reduce_scatter x5, waiting for transfers between devices, on_device(): lax.psum_scatter(partial_in.astype(jnp.bfloat16), 'tp', scatter_dimension...  290 us
    psum x5, blocking collectives, on_device(): stat = lax.psum(jnp.sum(dnorm_local * normed_local, axis=1), 'tp') / D  130 us
    ppermute x1, waiting for transfers between devices, from_behind(): lax.ppermute(array, axis, [(i, (i + by) % peers) for i in range(peers)])  81.6 us
    dot_general x30, matrix products, contract(): lax.dot_general(left, right, (((left_dim,), (right_dim,)), ((), ())), pre...  64.8 us
    slice x1, local copies, waits for them, and re-layouts, on_device(): new_down = averaged[2].reshape(wd.shape)[None, None]  32.6 us
  transfers between devices with their start and end apart: 19, of which 13 were waited for; matrix products, arithmetic and copies ran while one was open for 9% of the time, Pallas kernels for 0%

commit v1 on v0

--- a/solution.py
+++ b/solution.py
@@ -32,7 +32,9 @@
 
 
 def widen(value):
-    return lax.all_gather(value, "tp", axis=1, tiled=True)
+    return jnp.concatenate(
+        lax.all_to_all(jnp.stack([value] * lax.axis_size("tp")), "tp", 0, 0), axis=1
+    )
 
 
 def norm_parts(x_full):

time: 1540 us -> 1300 us (0.84)
  blocking collectives: 544 us -> 143 us
  waiting for transfers between devices: 729 us -> 800 us
  starting transfers between devices: 34.7 us -> 101 us
    all_gather x10 -> x0, blocking collectives: 414 us -> none  [widen(): return lax.all_gather(value, 'tp', axis=1, tiled=True)]
    all_to_all x0 -> x9, starting transfers between devices: none -> 66.3 us  [widen(): lax.all_to_all(jnp.stack([value] * lax.axis_size('tp')), 'tp', 0, 0)]
    all_to_all x0 -> x9, waiting for transfers between devices: none -> 63.2 us  [widen(): lax.all_to_all(jnp.stack([value] * lax.axis_size('tp')), 'tp', 0, 0)]
    all_to_all x0 -> x1, blocking collectives: none -> 18.1 us  [widen(): lax.all_to_all(jnp.stack([value] * lax.axis_size('tp')), 'tp', 0, 0)]
  transfers between devices with their start and end apart: 19 -> 28, of which waited for: 13 -> 24; matrix products, arithmetic and copies ran while one was open for 9% -> 13% of each run, Pallas kernels for 0% -> 0%
where the time goes in v1:
time: 1300 us; the launch traced here: 1280 us
  waiting for transfers between devices  800 us (62%)
  blocking collectives  143 us (11%)
  starting transfers between devices  101 us (8%)
  local copies, waits for them, and re-layouts  100 us (8%)
  matrix products  89 us (7%)
  other arithmetic  33.6 us (3%)
  between operations  16 us (1%)
    reduce_scatter x5, waiting for transfers between devices, on_device(): lax.psum_scatter(partial_out.astype(jnp.bfloat16), 'tp', scatter_dimensio...  356 us
    reduce_scatter x5, waiting for transfers between devices, on_device(): lax.psum_scatter(partial_in.astype(jnp.bfloat16), 'tp', scatter_dimension...  278 us
    psum x5, blocking collectives, on_device(): stat = lax.psum(jnp.sum(dnorm_local * normed_local, axis=1), 'tp') / D  125 us
    ppermute x1, waiting for transfers between devices, from_behind(): lax.ppermute(array, axis, [(i, (i + by) % peers) for i in range(peers)])  87.7 us
    dot_general x30, matrix products, contract(): lax.dot_general(left, right, (((left_dim,), (right_dim,)), ((), ())), pre...  68.3 us
    all_to_all x9, starting transfers between devices, widen(): lax.all_to_all(jnp.stack([value] * lax.axis_size('tp')), 'tp', 0, 0)  66.3 us
    all_to_all x9, waiting for transfers between devices, widen(): lax.all_to_all(jnp.stack([value] * lax.axis_size('tp')), 'tp', 0, 0)  63.2 us
    slice x1, local copies, waits for them, and re-layouts, on_device(): new_down = averaged[2].reshape(wd.shape)[None, None]  32.7 us
  transfers between devices with their start and end apart: 28, of which 24 were waited for; matrix products, arithmetic and copies ran while one was open for 13% of the time, Pallas kernels for 0%

profile of v1, /device:TPU:66, one launch (start us, length us, event | category | flops | bytes accessed | tf_op | source)
XLA Modules:
  0.0 1283.6 jit_solution(10124385350771374576)
XLA Ops:
  19.6 11.5 all-to-all-done
  35.2 72.2 %reduce-scatter.11.cloned.1.call-done = bf16[128,112]{0,1:T(8,128)(2,1)} async-done(((bf16[128,896]{0,1:T(8,128)(2,1)}), bf16[128,112]{0,1:T(8,128)(2,1)}) %reduce-scatter.11.cloned.1.call-update) | async-done | bytes 28688 | tf_op jit(solution)/shard_map/reduce_scatter | solution.py:108
  120.5 9.9 all-to-all-done.1
  134.6 72.4 %reduce-scatter.13.cloned.1.call-done = bf16[128,112]{0,1:T(8,128)(2,1)} async-done(((bf16[128,896]{0,1:T(8,128)(2,1)}), bf16[128,112]{0,1:T(8,128)(2,1)}) %reduce-scatter.13.cloned.1.call-update) | async-done | bytes 28688 | tf_op jit(solution)/shard_map/reduce_scatter | solution.py:108
  220.1 9.9 all-to-all-done.2
  234.2 72.4 %reduce-scatter.15.cloned.1.call-done = bf16[128,112]{0,1:T(8,128)(2,1)} async-done(((bf16[128,896]{0,1:T(8,128)(2,1)}), bf16[128,112]{0,1:T(8,128)(2,1)}) %reduce-scatter.15.cloned.1.call-update) | async-done | bytes 28688 | tf_op jit(solution)/shard_map/reduce_scatter | solution.py:108
  336.1 70.8 %reduce-scatter.17.cloned.1.call-done = bf16[128,112]{0,1:T(8,128)(2,1)} async-done(((bf16[128,896]{0,1:T(8,128)(2,1)}), bf16[128,112]{0,1:T(8,128)(2,1)}) %reduce-scatter.17.cloned.1.call-update) | async-done | bytes 28688 | tf_op jit(solution)/shard_map/reduce_scatter | solution.py:108
  453.5 70.8 %reduce-scatter.21.cloned.1.call-done = bf16[128,112]{0,1:T(8,128)(2,1)} async-done(((bf16[128,896]{0,1:T(8,128)(2,1)}), bf16[128,112]{0,1:T(8,128)(2,1)}) %reduce-scatter.21.cloned.1.call-update) | async-done | bytes 28688 | tf_op jit(solution)/shard_map/reduce_scatter | solution.py:154
  525.2 24.6 %psum.35 = f32[128]{0:T(128)S(1)} all-reduce(f32[128]{0:T(128)S(1)} %fusion.176), channel_id=1, replica_groups=mesh['section'=4,'rep'=8,'tp'=8] {'tp'}, use_global_device_ids=true, to_apply=%region_13.14 | all-reduce | flops 128 | bytes 1024 | tf_op jit(solution)/shard_map/psum | solution.py:158
  557.1 18.1 %all_to_all.50 = bf16[8,128,112]{1,2,0:T(8,128)(2,1)S(1)} all-to-all(bf16[8,128,112]{1,2,0:T(8,128)(2,1)S(1)} %stack.34), channel_id=1, replica_groups=mesh['section'=4,'rep'=8,'tp'=8] {'tp'}, dimensions={0} | all-to-all | bytes 458752 | tf_op jit(solution)/shard_map/all_to_all | solution.py:36
  583.0 69.0 %reduce-scatter.23.cloned.1.call-done = bf16[128,112]{0,1:T(8,128)(2,1)} async-done(((bf16[128,896]{0,1:T(8,128)(2,1)}), bf16[128,112]{0,1:T(8,128)(2,1)}) %reduce-scatter.23.cloned.1.call-update) | async-done | bytes 28688 | tf_op jit(solution)/shard_map/reduce_scatter | solution.py:154
  653.3 25.2 %psum.36 = f32[128]{0:T(128)} all-reduce(f32[128]{0:T(128)} %fusion.180), channel_id=1, replica_groups=mesh['section'=4,'rep'=8,'tp'=8] {'tp'}, use_global_device_ids=true, to_apply=%region_17.18 | all-reduce | flops 128 | bytes 1024 | tf_op jit(solution)/shard_map/psum | solution.py:158
  710.4 68.3 %reduce-scatter.19.cloned.1.call-done = bf16[128,112]{0,1:T(8,128)(2,1)} async-done(((bf16[128,896]{0,1:T(8,128)(2,1)}), bf16[128,112]{0,1:T(8,128)(2,1)}) %reduce-scatter.19.cloned.1.call-update) | async-done | bytes 28688 | tf_op jit(solution)/shard_map/reduce_scatter | solution.py:108
  785.7 70.2 %reduce-scatter.25.cloned.1.call-done = bf16[128,112]{0,1:T(8,128)(2,1)} async-done(((bf16[128,896]{0,1:T(8,128)(2,1)}), bf16[128,112]{0,1:T(8,128)(2,1)}) %reduce-scatter.25.cloned.1.call-update) | async-done | bytes 28688 | tf_op jit(solution)/shard_map/reduce_scatter | solution.py:154
  856.9 24.6 %psum.37 = f32[128]{0:T(128)S(1)} all-reduce(f32[128]{0:T(128)S(1)} %fusion.184), channel_id=1, replica_groups=mesh['section'=4,'rep'=8,'tp'=8] {'tp'}, use_global_device_ids=true, to_apply=%region_21.22 | all-reduce | flops 128 | bytes 1024 | tf_op jit(solution)/shard_map/psum | solution.py:158
  917.4 67.8 %reduce-scatter.27.cloned.1.call-done = bf16[128,112]{0,1:T(8,128)(2,1)} async-done(((bf16[128,896]{0,1:T(8,128)(2,1)}), bf16[128,112]{0,1:T(8,128)(2,1)}) %reduce-scatter.27.cloned.1.call-update) | async-done | bytes 28688 | tf_op jit(solution)/shard_map/reduce_scatter | solution.py:154
  986.1 25.1 %psum.38 = f32[128]{0:T(128)} all-reduce(f32[128]{0:T(128)S(1)} %fusion.188), channel_id=1, replica_groups=mesh['section'=4,'rep'=8,'tp'=8] {'tp'}, use_global_device_ids=true, to_apply=%region_25.26 | all-reduce | flops 128 | bytes 1024 | tf_op jit(solution)/shard_map/psum | solution.py:158
  1062.8 13.2 %stack_reshape.10 = bf16[1,544768]{1,0:T(2,128)(2,1)} reshape(bf16[544768]{0:T(1024)(128)(2,1)S(1)} %reshape.326) | data formatting | bytes 2179072 | tf_op jit(solution)/shard_map/stack;reshape | solution.py:171
  1086.4 11.3 stack_reshape.9
  1105.2 143.4 %conditional.2 = (bf16[3,544768]{1,0:T(4,128)(2,1)}, bf16[1,544768]{1,0:T(2,128)(2,1)}, bf16[1,544768]{1,0:T(2,128)(2,1)}, bf16[1,544768]{1,0:T(2,128)(2,1)}, bf...) conditional(s32[]{:T(128)} %clamp.3, ...), branch_computations={%region_30.31_spmd, %region_31.32_spmd, %region_32.33_spmd} | conditional | flops 8171520 | bytes 56655996
  1105.4 10.7 collective-permute-start.2
  1116.1 87.7 %collective-permute-done.2 = bf16[3,544768]{1,0:T(4,128)(2,1)S(1)} collective-permute-done((bf16[3,544768]{1,0:T(4,128)(2,1)S(1)}, bf16[3,544768]{1,0:T(4,128)(2,1)S(1)}, u32[]{:S(2)}, u32[]{:S(2)}) %collective-permute-start.2) | collective-permute-done | bytes 3268640 | tf_op jit(solution)/shard_map/cond/branch_2_fun/ppermute | solution.py:25
  1206.8 32.7 %fusion.231 = (bf16[544768]{0:T(1024)(128)(2,1)S(1)}, bf16[1,544768]{1,0:T(2,128)(2,1)}, bf16[544768]{0:T(1024)(128)(2,1)}, bf16[1,544768]{1,0:T(2,128)(2,1)}, b...) fusion(bf16[3,544768]{1,0:T(4,128)(2,1)S(1)} %add_multiply_fusion.2), kind=kLoop, calls=%fused_computation.391 | loop fusion | bytes 9805824 | tf_op jit(solution)/shard_map/slice | solution.py:184
  1249.6 25.3 %psum.39 = f32[128]{0:T(128)S(1)} all-reduce(f32[128]{0:T(128)S(1)} %fusion.192), channel_id=1, replica_groups=mesh['section'=4,'rep'=8,'tp'=8] {'tp'}, use_global_device_ids=true, to_apply=%region_29.30 | all-reduce | flops 128 | bytes 1024 | tf_op jit(solution)/shard_map/psum | solution.py:158
  (298 shorter events, 303.5 us)
Async XLA Ops:
  9.8 21.3 %all-to-all-start = ((bf16[8,128,112]{1,2,0:T(8,128)(2,1)}), bf16[8,128,112]{1,2,0:T(8,128)(2,1)S(1)}, u32[]{:S(2)}, u32[]{:S(2)}) async-start(bf16[8,128,112]{1,2,0:T(8,128)(2,1)} %stack.28), calls=%async_computation | async-start | bytes 458752 | tf_op jit(solution)/shard_map/all_to_all | solution.py:36
  19.6 87.8 %reduce-scatter.11.cloned.1.call-start = ((), (), s32[]{:S(2)}) async-start(), calls=%async_computation.20 | async-start | bytes 258048 | tf_op jit(solution)/shard_map/reduce_scatter | solution.py:108
  114.6 15.8 %all-to-all-start.1 = ((bf16[8,128,112]{1,2,0:T(8,128)(2,1)}), bf16[8,128,112]{1,2,0:T(8,128)(2,1)S(1)}, u32[]{:S(2)}, u32[]{:S(2)}) async-start(bf16[8,128,112]{1,2,0:T(8,128)(2,1)} %stack.29), calls=%async_computation.2 | async-start | bytes 458752 | tf_op jit(solution)/shard_map/all_to_all | solution.py:36
  120.5 86.4 %reduce-scatter.13.cloned.1.call-start = ((), (), s32[]{:S(2)}) async-start(), calls=%async_computation.21 | async-start | bytes 258048 | tf_op jit(solution)/shard_map/reduce_scatter | solution.py:108
  214.2 15.8 %all-to-all-start.2 = ((bf16[8,128,112]{1,2,0:T(8,128)(2,1)}), bf16[8,128,112]{1,2,0:T(8,128)(2,1)S(1)}, u32[]{:S(2)}, u32[]{:S(2)}) async-start(bf16[8,128,112]{1,2,0:T(8,128)(2,1)} %stack.30), calls=%async_computation.4 | async-start | bytes 458752 | tf_op jit(solution)/shard_map/all_to_all | solution.py:36
  220.1 86.4 %reduce-scatter.15.cloned.1.call-start = ((), (), s32[]{:S(2)}) async-start(), calls=%async_computation.22 | async-start | bytes 258048 | tf_op jit(solution)/shard_map/reduce_scatter | solution.py:108
  307.3 5.8 collective-permute-start.5
  314.6 15.8 %all-to-all-start.3 = ((bf16[8,128,112]{1,2,0:T(8,128)(2,1)}), bf16[8,128,112]{1,2,0:T(8,128)(2,1)S(1)}, u32[]{:S(2)}, u32[]{:S(2)}) async-start(bf16[8,128,112]{1,2,0:T(8,128)(2,1)} %stack.31), calls=%async_computation.6 | async-start | bytes 458752 | tf_op jit(solution)/shard_map/all_to_all | solution.py:36
  320.5 86.4 %reduce-scatter.17.cloned.1.call-start = ((), (), s32[]{:S(2)}) async-start(), calls=%async_computation.23 | async-start | bytes 258048 | tf_op jit(solution)/shard_map/reduce_scatter | solution.py:108
  415.1 15.8 %all-to-all-start.4 = ((bf16[8,128,112]{1,2,0:T(8,128)(2,1)}), bf16[8,128,112]{1,2,0:T(8,128)(2,1)S(1)}, u32[]{:S(2)}, u32[]{:S(2)}) async-start(bf16[8,128,112]{1,2,0:T(8,128)(2,1)} %stack.32), calls=%async_computation.8 | async-start | bytes 458752 | tf_op jit(solution)/shard_map/all_to_all | solution.py:36
  432.4 15.1 %all-to-all-start.5 = ((bf16[8,128,112]{1,2,0:T(8,128)(2,1)}), bf16[8,128,112]{1,2,0:T(8,128)(2,1)}, u32[]{:S(2)}, u32[]{:S(2)}) async-start(bf16[8,128,112]{1,2,0:T(8,128)(2,1)} %stack.33), calls=%async_computation.10 | async-start | bytes 458752 | tf_op jit(solution)/shard_map/all_to_all | solution.py:36
  438.1 86.2 %reduce-scatter.21.cloned.1.call-start = ((), (), s32[]{:S(2)}) async-start(), calls=%async_computation.25 | async-start | bytes 258048 | tf_op jit(solution)/shard_map/reduce_scatter | solution.py:154
  451.9 200.0 %reduce-scatter.23.cloned.1.call-start = ((), (), s32[]{:S(2)}) async-start(), calls=%async_computation.26 | async-start | bytes 258048 | tf_op jit(solution)/shard_map/reduce_scatter | solution.py:154
  680.1 6.0 collective-permute-start.8
  687.5 18.4 %all-to-all-start.7 = ((bf16[8,128,112]{1,2,0:T(8,128)(2,1)}), bf16[8,128,112]{1,2,0:T(8,128)(2,1)}, u32[]{:S(2)}, u32[]{:S(2)}) async-start(bf16[8,128,112]{1,2,0:T(8,128)(2,1)} %stack.35), calls=%async_computation.14 | async-start | bytes 458752 | tf_op jit(solution)/shard_map/all_to_all | solution.py:36
  696.5 82.1 %reduce-scatter.19.cloned.1.call-start = ((), (), s32[]{:S(2)}) async-start(), calls=%async_computation.24 | async-start | bytes 258048 | tf_op jit(solution)/shard_map/reduce_scatter | solution.py:108
  699.3 156.7 %reduce-scatter.25.cloned.1.call-start = ((), (), s32[]{:S(2)}) async-start(), calls=%async_computation.27 | async-start | bytes 258048 | tf_op jit(solution)/shard_map/reduce_scatter | solution.py:154
  882.3 6.0 collective-permute-start.9
  889.1 18.3 %all-to-all-start.8 = ((bf16[8,128,112]{1,2,0:T(8,128)(2,1)}), bf16[8,128,112]{1,2,0:T(8,128)(2,1)S(1)}, u32[]{:S(2)}, u32[]{:S(2)}) async-start(bf16[8,128,112]{1,2,0:T(8,128)(2,1)} %stack.36), calls=%async_computation.16 | async-start | bytes 458752 | tf_op jit(solution)/shard_map/all_to_all | solution.py:36
  898.1 87.1 %reduce-scatter.27.cloned.1.call-start = ((), (), s32[]{:S(2)}) async-start(), calls=%async_computation.28 | async-start | bytes 258048 | tf_op jit(solution)/shard_map/reduce_scatter | solution.py:154
  1012.7 6.1 collective-permute-start.10
  1020.1 18.4 %all-to-all-start.9 = ((bf16[8,128,112]{1,2,0:T(8,128)(2,1)}), bf16[8,128,112]{1,2,0:T(8,128)(2,1)}, u32[]{:S(2)}, u32[]{:S(2)}) async-start(bf16[8,128,112]{1,2,0:T(8,128)(2,1)} %stack.37), calls=%async_computation.18 | async-start | bytes 458752 | tf_op jit(solution)/shard_map/all_to_all | solution.py:36
  1029.2 219.4 %reduce-scatter.29.cloned.1.call-start = ((), (), s32[]{:S(2)}) async-start(), calls=%async_computation.29 | async-start | bytes 258048 | tf_op jit(solution)/shard_map/reduce_scatter | solution.py:154
  1105.4 98.5 %collective-permute-start.2 = (bf16[3,544768]{1,0:T(4,128)(2,1)S(1)}, bf16[3,544768]{1,0:T(4,128)(2,1)S(1)}, u32[]{:S(2)}, u32[]{:S(2)}) collective-permute-start(bf16[3,544768]{1,0:T(4,128)(2,1)S(1)} %param.2), channel_id=1, source_target_pairs={{0,32},{8,40},{16,48},{24,56},{32,0},{40,8},{48,16},{56,24},{1,33}... | collective-permute-start | bytes 9805832 | tf_op jit(solution)/shard_map/cond/branch_2_fun/ppermute | solution.py:25
  (59 other events, 1361.5 us)
Sparse Core Ops, SparseCore 0:
  35.3 71.9 reduce-scatter.10
  134.7 72.1 reduce-scatter.12
  234.3 72.1 reduce-scatter.14
  334.7 72.2 reduce-scatter.16
  452.0 72.1 reduce-scatter.20
  579.6 72.2 reduce-scatter.22
  701.6 76.9 reduce-scatter.18
  782.8 73.0 reduce-scatter.24
  911.8 73.3 reduce-scatter.26
  1042.6 73.2 reduce-scatter.28
